TPU v7x, 32 devices: a whole 2x2x4 slice. The times are simulated.
32 devices in a mesh: section: 2 (over core), seq: 16 (over z, y, x).
Axes of the slice: x: 2, y: 2, z: 4, core: 2. Of those that a mesh axis runs over, the one named last changes fastest.
Arguments:
- tokens: bfloat16 [1, 2048, 1024], P(None, 'seq'), may hold values from -24 to 24
- neighbor_ids: int32 [16, 9], P('seq'), may hold values from 0 to 15, as said below
- neighbor_count: int32 [16], P('seq'), may hold values from 1 to 9, as said below
- w_query: bfloat16 [2, 1024, 1024], P('section')
- w_key: bfloat16 [2, 1024, 1024], P('section')
- w_value: bfloat16 [2, 1024, 1024], P('section'), may hold values from -0.1875 to 0.1875
- w_out: bfloat16 [2, 1024, 1024], P('section'), may hold values from -0.1875 to 0.1875
- norm_gain: float32 [2, 1024], P('section'), may hold values from 0.5 to 3
- w_up: bfloat16 [2, 4096, 1024], P('section', 'seq'), may hold values from -0.1875 to 0.1875
- w_down: bfloat16 [2, 4096, 1024], P('section', 'seq'), may hold values from -0.09375 to 0.09375
- mlp_gain: float32 [2, 1024], P('section'), may hold values from 0.5 to 2
Outputs:
- layer_outputs: bfloat16 [2, 1, 2048, 1024], P('section', None, 'seq')
Inputs may be any that keep to these rules, and one draw needn't show every extreme that they name: `neighbor_ids`: blocks lie row by row on a map 4 blocks wide. Row b lists in its first neighbor_count[b] entries distinct blocks among b and the up to eight blocks beside it on the map (diagonals included), b first; its other entries equal b. `neighbor_count`: some block has 9.
All inputs are finite; a program needn't handle non-finite values.
Results may differ from a plain program's by a relative error of at most 0.017.
Values may be sent and summed in bfloat16 or wider, within the bound.
A program may use at most 128 MiB of HBM per device.

v0:
```python
import math
import jax
import jax.numpy as jnp
from jax import lax
from jax.sharding import PartitionSpec as P

HEADS = 16
BLK = 128
ROW = 4


def from_behind(block, axis, distance):
    devices = range(lax.axis_size(axis))
    route = [(i - distance, i) for i in devices if i - distance in devices]
    return lax.ppermute(block, axis, route)


def fetch_band(packed, reach_count):
    blocks_here = packed.shape[0]
    distances = [0, 1, -1, ROW - 1, 1 - ROW, ROW, -ROW, ROW + 1, -ROW - 1]
    wanted = set(
        (
            (position + jump_size) // blocks_here
            for position in range(blocks_here)
            for jump_size in distances
        )
    )
    pieces = []
    for offset in range(-reach_count, reach_count + 1):
        if offset == 0:
            pieces.append(packed)
        elif offset in wanted:
            pieces.append(from_behind(packed, "seq", -offset))
        else:
            pieces.append(jnp.zeros_like(packed))
    return jnp.concatenate(pieces, axis=0)


def soft_weights(scores, live, score_scale):
    scaled = jnp.where(live, scores * score_scale, -jnp.inf)
    row_max = jnp.max(scaled, axis=-1, keepdims=True)
    exponent = jnp.exp(scaled - row_max)
    return (exponent / jnp.sum(exponent, axis=-1, keepdims=True)).astype(jnp.bfloat16)


def rms_normed(widened, gain):
    return (
        widened * lax.rsqrt(jnp.mean(widened * widened, axis=-1, keepdims=True) + 1e-05) * gain
    ).astype(jnp.bfloat16)


def prepare(inputs, gain, query_weight, key_weight, value_weight):
    tok_rows, width = inputs.shape
    normed = rms_normed(inputs.astype(jnp.float32), gain)
    queries = jnp.dot(normed, query_weight, preferred_element_type=jnp.float32).astype(jnp.bfloat16)
    keys = jnp.dot(normed, key_weight, preferred_element_type=jnp.float32).astype(jnp.bfloat16)
    values = jnp.dot(normed, value_weight, preferred_element_type=jnp.float32).astype(jnp.bfloat16)
    packed = jnp.concatenate([keys, values], axis=-1).reshape(tok_rows // BLK, BLK, 2 * width)
    return (queries, packed)


def finish(
    inputs,
    queries,
    band_rows,
    neighbor_ids,
    neighbor_count,
    out_weight,
    up_weight,
    down_weight,
    second_gain,
    device,
    reach_count,
):
    tok_rows, width = inputs.shape
    blocks_here = tok_rows // BLK
    slot_total = neighbor_ids.shape[1]
    head_size = width // HEADS
    score_scale = 1.0 / math.sqrt(head_size)
    band_start = (device - reach_count) * blocks_here
    slot_live = jnp.arange(slot_total, dtype=jnp.int32)[None, :] < neighbor_count[:, None]
    query_blocks = queries.reshape(blocks_here, BLK, HEADS, head_size)
    band_keys = band_rows[..., :width]
    band_values = band_rows[..., width:]
    local_ids = neighbor_ids - band_start
    key_set = jnp.take(band_keys, local_ids, axis=0).reshape(
        blocks_here, slot_total * BLK, HEADS, head_size
    )
    value_set = jnp.take(band_values, local_ids, axis=0).reshape(
        blocks_here, slot_total * BLK, HEADS, head_size
    )
    key_live = jnp.repeat(slot_live, BLK, axis=1)
    scores = jnp.einsum(
        "bqhd,bkhd->bhqk", query_blocks, key_set, preferred_element_type=jnp.float32
    )
    probs = soft_weights(scores, key_live[:, None, None, :], score_scale)
    mixed = jnp.einsum(
        "bhqk,bkhd->bqhd", probs, value_set, preferred_element_type=jnp.float32
    ).astype(jnp.bfloat16)
    mixed = mixed.reshape(tok_rows, width)
    attended = (
        inputs.astype(jnp.float32) + jnp.dot(mixed, out_weight, preferred_element_type=jnp.float32)
    ).astype(jnp.bfloat16)
    attended_wide = attended.astype(jnp.float32)
    second = rms_normed(attended_wide, second_gain)
    upper_rows = lax.dot_general(
        second, up_weight, (((1,), (1,)), ((), ())), preferred_element_type=jnp.float32
    )
    hidden = jax.nn.gelu(upper_rows, approximate=True).astype(jnp.bfloat16)
    return (
        attended_wide + jnp.dot(hidden, down_weight, preferred_element_type=jnp.float32)
    ).astype(jnp.bfloat16)


def local(
    tokens,
    neighbor_ids,
    neighbor_count,
    w_query,
    w_key,
    w_value,
    w_out,
    norm_gain,
    w_up,
    w_down,
    mlp_gain,
):
    graphs, tok_rows, width = tokens.shape
    blocks_here = tok_rows // BLK
    reach_count = (ROW + blocks_here) // blocks_here
    sections = lax.axis_size("section")
    section_index = lax.axis_index("section")
    device = lax.axis_index("seq")
    ticks = graphs + sections - 1
    up_whole, down_whole = (
        lax.all_gather(w_up, "seq", axis=1, tiled=True),
        lax.all_gather(w_down, "seq", axis=1, tiled=True),
    )
    results = jnp.zeros((1, graphs, tok_rows, width), jnp.bfloat16)
    incoming = jnp.zeros((tok_rows, width), jnp.bfloat16)
    for tick_index in range(ticks):
        first_input = tokens[min(tick_index, graphs - 1)]
        layer_input = jnp.where(section_index == 0, first_input, incoming)
        graph_index = tick_index - section_index
        active = (graph_index >= 0) & (graph_index < graphs)

        def run_prepare(operand_rows):
            return prepare(operand_rows, norm_gain[0], w_query[0], w_key[0], w_value[0])

        def skip_prepare(operand_rows):
            return (
                jnp.zeros((tok_rows, width), jnp.bfloat16),
                jnp.zeros((blocks_here, BLK, 2 * width), jnp.bfloat16),
            )

        queries, packed = lax.cond(active, run_prepare, skip_prepare, layer_input)
        band_rows = fetch_band(packed, reach_count)

        def run_finish(operand_set):
            return finish(
                operand_set[0],
                operand_set[1],
                operand_set[2],
                neighbor_ids,
                neighbor_count,
                w_out[0],
                up_whole[0],
                down_whole[0],
                mlp_gain[0],
                device,
                reach_count,
            )

        def skip_finish(operand_set):
            return jnp.zeros((tok_rows, width), jnp.bfloat16)

        layer_output = lax.cond(active, run_finish, skip_finish, (layer_input, queries, band_rows))
        results = results.at[0, 0].set(jnp.where(graph_index == 0, layer_output, results[0, 0]))
        if tick_index + 1 < ticks:
            incoming = from_behind(layer_output, "section", 1)
    return results


def solution(mesh):
    in_specs = (
        P(None, "seq", None),
        P("seq", None),
        P("seq"),
        P("section", None, None),
        P("section", None, None),
        P("section", None, None),
        P("section", None, None),
        P("section", None),
        P("section", "seq", None),
        P("section", "seq", None),
        P("section", None),
    )
    out_specs = P("section", None, "seq", None)
    return jax.shard_map(local, mesh=mesh, in_specs=in_specs, out_specs=out_specs, check_vma=False)
```

profile of v0, /device:TPU:9, one launch (start us, length us, event | category | flops | bytes accessed | tf_op | source)
XLA Modules:
  0.0 490.4 jit_solution(1373884698683510926)
XLA Ops:
  8.0 1.0 bitcast_select_fusion.5
  9.1 4.2 collective-permute-start
  13.3 3.2 collective-permute-start.1
  16.5 2.8 collective-permute-start.2
  19.3 2.2 collective-permute-start.3
  21.5 4.8 collective-permute-start.4
  26.4 3.0 collective-permute-start.5
  30.2 10.4 %collective-permute-done.1 = bf16[1,128,2048]{2,1,0:T(8,128)(2,1)} collective-permute-done((bf16[1,128,2048]{2,1,0:T(8,128)(2,1)S(1)}, bf16[1,128,2048]{2,1,0:T(8,128)(2,1)}, u32[]{:S(2)}, u32[]{:S(2)}) %collective-permute-start.1) | collective-permute-done | bytes 524320 | tf_op jit(solution)/shard_map/ppermute | solution.py:15
  40.6 1.9 collective-permute-start.6
  42.5 1.9 constant_dynamic-update-slice_fusion.7
  44.4 17.4 %collective-permute-done.2 = bf16[1,128,2048]{2,1,0:T(8,128)(2,1)} collective-permute-done((bf16[1,128,2048]{2,1,0:T(8,128)(2,1)S(1)}, bf16[1,128,2048]{2,1,0:T(8,128)(2,1)}, u32[]{:S(2)}, u32[]{:S(2)}) %collective-permute-start.2) | collective-permute-done | bytes 524320 | tf_op jit(solution)/shard_map/ppermute | solution.py:15
  61.8 1.3 collective-permute-start.7
  63.1 1.9 constant_dynamic-update-slice_fusion.6
  65.0 0.8 broadcast_dynamic-update-slice_fusion
  65.9 19.2 %collective-permute-done.3 = bf16[1,128,2048]{2,1,0:T(8,128)(2,1)S(1)} collective-permute-done((bf16[1,128,2048]{2,1,0:T(8,128)(2,1)S(1)}, bf16[1,128,2048]{2,1,0:T(8,128)(2,1)S(1)}, u32[]{:S(2)}, u32[]{:S(2)}) %collective-permute-start.3) | collective-permute-done | bytes 524320 | tf_op jit(solution)/shard_map/ppermute | solution.py:15
  85.0 0.8 constant_dynamic-update-slice_fusion.5
  85.9 0.9 constant_dynamic-update-slice_fusion.4
  86.7 8.9 %collective-permute-done.4 = bf16[1,128,2048]{2,1,0:T(8,128)(2,1)S(1)} collective-permute-done((bf16[1,128,2048]{2,1,0:T(8,128)(2,1)S(1)}, bf16[1,128,2048]{2,1,0:T(8,128)(2,1)S(1)}, u32[]{:S(2)}, u32[]{:S(2)}) %collective-permute-start.4) | collective-permute-done | bytes 524320 | tf_op jit(solution)/shard_map/ppermute | solution.py:15
  95.6 0.9 constant_dynamic-update-slice_fusion.3
  96.5 0.8 broadcast_dynamic-update-slice_fusion.3
  97.3 0.8 constant_dynamic-update-slice_fusion.2
  98.2 0.8 constant_dynamic-update-slice_fusion.1
  99.0 0.8 constant_dynamic-update-slice_fusion
  99.9 67.9 %all-gather.3.cloned.1.call-done = bf16[1,4096,1024]{2,1,0:T(8,128)(2,1)} async-done(((bf16[1,256,1024]{2,1,0:T(8,128)(2,1)}), bf16[1,4096,1024]{2,1,0:T(8,128)(2,1)}) %all-gather.3.cloned.1.call-update) | async-done | bytes 8388624 | tf_op jit(solution)/shard_map/all_gather | solution.py:136
  167.8 113.8 %all-gather.5.cloned.1.call-done = bf16[1,4096,1024]{2,1,0:T(8,128)(2,1)} async-done(((bf16[1,256,1024]{2,1,0:T(8,128)(2,1)}), bf16[1,4096,1024]{2,1,0:T(8,128)(2,1)}) %all-gather.5.cloned.1.call-update) | async-done | bytes 8388624 | tf_op jit(solution)/shard_map/all_gather | solution.py:137
  281.9 1.3 collective-permute-start.8
  283.2 60.4 %collective-permute-done.8 = bf16[128,1024]{1,0:T(8,128)(2,1)S(1)} collective-permute-done((bf16[128,1024]{1,0:T(8,128)(2,1)S(1)}, bf16[128,1024]{1,0:T(8,128)(2,1)S(1)}, u32[]{:S(2)}, u32[]{:S(2)}) %collective-permute-start.8) | collective-permute-done | bytes 262176 | tf_op jit(solution)/shard_map/ppermute | solution.py:15
  343.6 1.0 bitcast_select_fusion.4
  344.6 5.0 %conditional.6 = (bf16[128,1024]{1,0:T(8,128)(2,1)S(1)}, bf16[1,128,2048]{2,1,0:T(8,128)(2,1)S(1)}) conditional(s32[]{:T(128)} %convert_element_type.100, () %tuple.47, (bf16[128,1024]{1,0:T(8,128)(2,1)S(1)}, f32[1,1024]{1,0:T(1,128)S(1)}, bf16[1,1024,1024]{2,1,0:T(8,128)(2,1)}, bf16[1,1024,1024]{2,1,0:T(8,128)(2,1)}, ...), branch_computations={%region_8.10_spmd, %region_9.12_spmd} | conditional | flops 808714368 | bytes 17579052 | solution.py:156
  344.7 2.2 fusion.30
  346.9 2.1 fusion.33
  349.6 4.1 collective-permute-start.9
  353.7 2.1 collective-permute-start.10
  355.8 3.0 collective-permute-start.11
  358.8 2.2 collective-permute-start.12
  361.1 4.9 collective-permute-start.13
  366.0 2.5 collective-permute-start.14
  369.3 3.8 collective-permute-done.10
  373.0 1.9 collective-permute-start.15
  375.0 0.9 constant_dynamic-update-slice_fusion.16
  375.8 20.2 %collective-permute-done.11 = bf16[1,128,2048]{2,1,0:T(8,128)(2,1)S(1)} collective-permute-done((bf16[1,128,2048]{2,1,0:T(8,128)(2,1)S(1)}, bf16[1,128,2048]{2,1,0:T(8,128)(2,1)S(1)}, u32[]{:S(2)}, u32[]{:S(2)}) %collective-permute-start.11) | collective-permute-done | bytes 524320 | tf_op jit(solution)/shard_map/ppermute | solution.py:15
  396.0 1.3 collective-permute-start.16
  397.3 0.9 constant_dynamic-update-slice_fusion.15
  398.2 0.8 broadcast_dynamic-update-slice_fusion.1
  399.0 18.0 %collective-permute-done.12 = bf16[1,128,2048]{2,1,0:T(8,128)(2,1)S(1)} collective-permute-done((bf16[1,128,2048]{2,1,0:T(8,128)(2,1)S(1)}, bf16[1,128,2048]{2,1,0:T(8,128)(2,1)S(1)}, u32[]{:S(2)}, u32[]{:S(2)}) %collective-permute-start.12) | collective-permute-done | bytes 524320 | tf_op jit(solution)/shard_map/ppermute | solution.py:15
  417.0 0.8 constant_dynamic-update-slice_fusion.14
  417.8 0.9 constant_dynamic-update-slice_fusion.13
  418.7 1.2 collective-permute-done.13
  419.8 0.9 constant_dynamic-update-slice_fusion.12
  420.7 0.8 broadcast_dynamic-update-slice_fusion.2
  421.6 0.8 constant_dynamic-update-slice_fusion.11
  422.4 0.8 constant_dynamic-update-slice_fusion.10
  423.2 0.8 constant_dynamic-update-slice_fusion.9
  424.1 58.7 %conditional.7 = (bf16[128,1024]{1,0:T(8,128)(2,1)S(1)}) conditional(s32[]{:T(128)} %convert_element_type.100, () %tuple.42, (bf16[128,1024]{1,0:T(8,128)(2,1)S(1)}, bf16[11,128,2048]{2,1,0:T(8,128)(2,1)}, s32[]{:T(128)}, s32[1,9]{1,0:T(1,128)S(1)}, s32[1]{0:T(128)}, /*index=5*/bf16[128,1024]{1,0:T(8,128)(2,1)S(1)}, ...), branch_computations={%region_11.13_spmd, %region_12.17_spmd} | conditional | flops 3047426304 | bytes 114586176 | solution.py:177
  424.8 5.2 %fusion.164 = (bf16[11,128,1024]{2,1,0:T(8,128)(2,1)}, bf16[11,128,1024]{2,1,0:T(8,128)(2,1)S(1)}) fusion(bf16[11,128,2048]{2,1,0:T(8,128)(2,1)} %get-tuple-element.117), kind=kLoop, calls=%fused_computation.169 | loop fusion | bytes 11534336 | tf_op jit(solution)/shard_map/cond/branch_1_fun/slice | solution.py:84
  430.0 4.1 gather_fusion.2
  434.1 2.4 gather_fusion.3
  436.5 4.3 bitcast_select_fusion.3
  440.8 7.3 %reshape.288 = bf16[1152,16,64]{2,1,0:T(8,128)(2,1)} reshape(bf16[1,9,128,1024]{3,2,1,0:T(8,128)(2,1)} %get-tuple-element.189) | data formatting | bytes 4718592 | tf_op jit(solution)/shard_map/reshape.89
  448.3 3.2 fusion.111
  452.3 6.7 %fusion.165 = (f32[16,128]{1,0:T(8,128)S(1)}, f32[16,128,1152]{1,2,0:T(8,128)}) fusion(f32[16,1152,128]{2,1,0:T(8,128)S(1)} %fusion.111, pred[1152]{0:T(1024)(128)(4,1)S(1)} %broadcast_bitcast_fusion.1), kind=kOutput, calls=%fused_computation.170 | output fusion | flops 14156927 | bytes 18883712 | tf_op jit(solution)/shard_map/cond/branch_1_fun/sub | solution.py:42
  459.0 4.7 reshape.287
  463.7 8.2 %fusion.141 = bf16[16,64,128]{2,1,0:T(8,128)(2,1)S(1)} fusion(f32[16,128,1152]{1,2,0:T(8,128)} %get-tuple-element.191, f32[16,128]{1,0:T(8,128)S(1)} %get-tuple-element.190, bf16[1152,16,64]{2,1,0:T(8,128)(2,1)} %reshape.287), kind=kOutput, calls=%fused_computation.123 | convolution fusion | flops 306839552 | bytes 12066816 | tf_op jit(solution)/shard_map/cond/branch_1_fun/bhqk,bkhd->bqhd/dot_general | solution.py:97
  472.5 10.0 %fusion.138 = bf16[128,1024]{1,0:T(8,128)(2,1)S(1)} fusion(f32[128,1024]{1,0:T(8,128)S(1)} %get-tuple-element.193, bf16[1,4096,1024]{2,1,0:T(8,128)(2,1)} %get-tuple-element.125, bf16[1,4096,1024]{2,1,0:T(8,128)(2,1)} %get-tuple-element.124, f32[1024]{0:T(1024)S(1)} %bitcast.180, f32[128]{0:T(128)S(1)} %add_rsqrt_fusion.3), kind=kOutput, calls=%fused_computation.122 | convolution fusion | flops 2152857600 | bytes 17568256 | tf_op jit(solution)/shard_map/cond/branch_1_fun/dot_general | solution.py:111
  (49 shorter events, 7.1 us)
Async XLA Ops:
  6.5 161.2 %all-gather.3.cloned.1.call-start = ((), (), s32[]{:S(2)}) async-start(), calls=%async_computation | async-start | bytes 8912896 | tf_op jit(solution)/shard_map/all_gather | solution.py:136
  7.3 274.3 %all-gather.5.cloned.1.call-start = ((), (), s32[]{:S(2)}) async-start(), calls=%async_computation.1 | async-start | bytes 8912896 | tf_op jit(solution)/shard_map/all_gather | solution.py:137
  9.1 17.3 %collective-permute-start = (bf16[1,128,2048]{2,1,0:T(8,128)(2,1)S(1)}, bf16[1,128,2048]{2,1,0:T(8,128)(2,1)S(1)}, u32[]{:S(2)}, u32[]{:S(2)}) collective-permute-start(bf16[1,128,2048]{2,1,0:T(8,128)(2,1)S(1)} %get-tuple-element.130), channel_id=1, source_target_pairs={{0,5},{1,6},{2,7},{3,8},{4,9},{5,10},{6,11},{7,12},{8,13},{9,14},{... | collective-permute-start | bytes 1572872 | tf_op jit(solution)/shard_map/ppermute | solution.py:15
  13.3 27.3 %collective-permute-start.1 = (bf16[1,128,2048]{2,1,0:T(8,128)(2,1)S(1)}, bf16[1,128,2048]{2,1,0:T(8,128)(2,1)}, u32[]{:S(2)}, u32[]{:S(2)}) collective-permute-start(bf16[1,128,2048]{2,1,0:T(8,128)(2,1)S(1)} %get-tuple-element.130), channel_id=1, source_target_pairs={{0,4},{1,5},{2,6},{3,7},{4,8},{5,9},{6,10},{7,11},{8,12},{9,13},{1... | collective-permute-start | bytes 1572872 | tf_op jit(solution)/shard_map/ppermute | solution.py:15
  16.5 45.4 %collective-permute-start.2 = (bf16[1,128,2048]{2,1,0:T(8,128)(2,1)S(1)}, bf16[1,128,2048]{2,1,0:T(8,128)(2,1)}, u32[]{:S(2)}, u32[]{:S(2)}) collective-permute-start(bf16[1,128,2048]{2,1,0:T(8,128)(2,1)S(1)} %get-tuple-element.130), channel_id=1, source_target_pairs={{0,3},{1,4},{2,5},{3,6},{4,7},{5,8},{6,9},{7,10},{8,11},{9,12},{10... | collective-permute-start | bytes 1572872 | tf_op jit(solution)/shard_map/ppermute | solution.py:15
  19.3 65.8 %collective-permute-start.3 = (bf16[1,128,2048]{2,1,0:T(8,128)(2,1)S(1)}, bf16[1,128,2048]{2,1,0:T(8,128)(2,1)S(1)}, u32[]{:S(2)}, u32[]{:S(2)}) collective-permute-start(bf16[1,128,2048]{2,1,0:T(8,128)(2,1)S(1)} %get-tuple-element.130), channel_id=1, source_target_pairs={{0,1},{1,2},{2,3},{3,4},{4,5},{5,6},{6,7},{7,8},{8,9},{9,10},{10,1... | collective-permute-start | bytes 1572872 | tf_op jit(solution)/shard_map/ppermute | solution.py:15
  21.5 74.1 %collective-permute-start.4 = (bf16[1,128,2048]{2,1,0:T(8,128)(2,1)S(1)}, bf16[1,128,2048]{2,1,0:T(8,128)(2,1)S(1)}, u32[]{:S(2)}, u32[]{:S(2)}) collective-permute-start(bf16[1,128,2048]{2,1,0:T(8,128)(2,1)S(1)} %get-tuple-element.130), channel_id=1, source_target_pairs={{1,0},{2,1},{3,2},{4,3},{5,4},{6,5},{7,6},{8,7},{9,8},{10,9},{11,1... | collective-permute-start | bytes 1572872 | tf_op jit(solution)/shard_map/ppermute | solution.py:15
  26.4 71.0 %collective-permute-start.5 = (bf16[1,128,2048]{2,1,0:T(8,128)(2,1)S(1)}, bf16[1,128,2048]{2,1,0:T(8,128)(2,1)S(1)}, u32[]{:S(2)}, u32[]{:S(2)}) collective-permute-start(bf16[1,128,2048]{2,1,0:T(8,128)(2,1)S(1)} %get-tuple-element.130), channel_id=1, source_target_pairs={{3,0},{4,1},{5,2},{6,3},{7,4},{8,5},{9,6},{10,7},{11,8},{12,9},{13... | collective-permute-start | bytes 1572872 | tf_op jit(solution)/shard_map/ppermute | solution.py:15
  30.2 251.4 %copy-start.10 = (s32[1,9]{1,0:T(1,128)S(1)}, s32[1,9]{1,0:T(1,128)}, u32[]{:S(2)}) copy-start(s32[1,9]{1,0:T(1,128)} %param.26) | copy-start | bytes 112
  30.2 251.4 %copy-start.11 = (f32[1,1024]{1,0:T(1,128)S(1)}, f32[1,1024]{1,0:T(1,128)}, u32[]{:S(2)}) copy-start(f32[1,1024]{1,0:T(1,128)} %param.35) | copy-start | bytes 12292
  40.6 57.6 %collective-permute-start.6 = (bf16[1,128,2048]{2,1,0:T(8,128)(2,1)S(1)}, bf16[1,128,2048]{2,1,0:T(8,128)(2,1)S(1)}, u32[]{:S(2)}, u32[]{:S(2)}) collective-permute-start(bf16[1,128,2048]{2,1,0:T(8,128)(2,1)S(1)} %get-tuple-element.130), channel_id=1, source_target_pairs={{4,0},{5,1},{6,2},{7,3},{8,4},{9,5},{10,6},{11,7},{12,8},{13,9},{1... | collective-permute-start | bytes 1572872 | tf_op jit(solution)/shard_map/ppermute | solution.py:15
  61.8 37.2 %collective-permute-start.7 = (bf16[1,128,2048]{2,1,0:T(8,128)(2,1)S(1)}, bf16[1,128,2048]{2,1,0:T(8,128)(2,1)S(1)}, u32[]{:S(2)}, u32[]{:S(2)}) collective-permute-start(bf16[1,128,2048]{2,1,0:T(8,128)(2,1)S(1)} %get-tuple-element.130), channel_id=1, source_target_pairs={{5,0},{6,1},{7,2},{8,3},{9,4},{10,5},{11,6},{12,7},{13,8},{14,9},{... | collective-permute-start | bytes 1572872 | tf_op jit(solution)/shard_map/ppermute | solution.py:15
  281.6 63.0 %copy-start.8 = (f32[1,1024]{1,0:T(1,128)S(1)}, f32[1,1024]{1,0:T(1,128)}, u32[]{:S(2)}) copy-start(f32[1,1024]{1,0:T(1,128)} %param.32) | copy-start | bytes 12292
  281.8 62.7 %copy-start.4 = (bf16[128,1024]{1,0:T(8,128)(2,1)}, bf16[128,1024]{1,0:T(8,128)(2,1)S(1)}, u32[]{:S(2)}) copy-start(bf16[128,1024]{1,0:T(8,128)(2,1)S(1)} %get-tuple-element.202) | copy-start | bytes 786436
  281.9 61.7 %collective-permute-start.8 = (bf16[128,1024]{1,0:T(8,128)(2,1)S(1)}, bf16[128,1024]{1,0:T(8,128)(2,1)S(1)}, u32[]{:S(2)}, u32[]{:S(2)}) collective-permute-start(bf16[128,1024]{1,0:T(8,128)(2,1)S(1)} %get-tuple-element.202), channel_id=1, source_target_pairs={{0,16},{1,17},{2,18},{3,19},{4,20},{5,21},{6,22},{7,23},{8,24},{9,... | collective-permute-start | bytes 786440 | tf_op jit(solution)/shard_map/ppermute | solution.py:15
  344.6 4.5 copy-start.1
  349.6 16.4 %collective-permute-start.9 = (bf16[1,128,2048]{2,1,0:T(8,128)(2,1)S(1)}, bf16[1,128,2048]{2,1,0:T(8,128)(2,1)S(1)}, u32[]{:S(2)}, u32[]{:S(2)}) collective-permute-start(bf16[1,128,2048]{2,1,0:T(8,128)(2,1)S(1)} %get-tuple-element.132), channel_id=1, source_target_pairs={{0,5},{1,6},{2,7},{3,8},{4,9},{5,10},{6,11},{7,12},{8,13},{9,14},{... | collective-permute-start | bytes 1572872 | tf_op jit(solution)/shard_map/ppermute | solution.py:15
  353.7 19.3 %collective-permute-start.10 = (bf16[1,128,2048]{2,1,0:T(8,128)(2,1)S(1)}, bf16[1,128,2048]{2,1,0:T(8,128)(2,1)S(1)}, u32[]{:S(2)}, u32[]{:S(2)}) collective-permute-start(bf16[1,128,2048]{2,1,0:T(8,128)(2,1)S(1)} %get-tuple-element.132), channel_id=1, source_target_pairs={{0,4},{1,5},{2,6},{3,7},{4,8},{5,9},{6,10},{7,11},{8,12},{9,13},{1... | collective-permute-start | bytes 1572872 | tf_op jit(solution)/shard_map/ppermute | solution.py:15
  355.8 40.2 %collective-permute-start.11 = (bf16[1,128,2048]{2,1,0:T(8,128)(2,1)S(1)}, bf16[1,128,2048]{2,1,0:T(8,128)(2,1)S(1)}, u32[]{:S(2)}, u32[]{:S(2)}) collective-permute-start(bf16[1,128,2048]{2,1,0:T(8,128)(2,1)S(1)} %get-tuple-element.132), channel_id=1, source_target_pairs={{0,3},{1,4},{2,5},{3,6},{4,7},{5,8},{6,9},{7,10},{8,11},{9,12},{10... | collective-permute-start | bytes 1572872 | tf_op jit(solution)/shard_map/ppermute | solution.py:15
  358.8 58.1 %collective-permute-start.12 = (bf16[1,128,2048]{2,1,0:T(8,128)(2,1)S(1)}, bf16[1,128,2048]{2,1,0:T(8,128)(2,1)S(1)}, u32[]{:S(2)}, u32[]{:S(2)}) collective-permute-start(bf16[1,128,2048]{2,1,0:T(8,128)(2,1)S(1)} %get-tuple-element.132), channel_id=1, source_target_pairs={{0,1},{1,2},{2,3},{3,4},{4,5},{5,6},{6,7},{7,8},{8,9},{9,10},{10,1... | collective-permute-start | bytes 1572872 | tf_op jit(solution)/shard_map/ppermute | solution.py:15
  361.1 58.8 %collective-permute-start.13 = (bf16[1,128,2048]{2,1,0:T(8,128)(2,1)S(1)}, bf16[1,128,2048]{2,1,0:T(8,128)(2,1)S(1)}, u32[]{:S(2)}, u32[]{:S(2)}) collective-permute-start(bf16[1,128,2048]{2,1,0:T(8,128)(2,1)S(1)} %get-tuple-element.132), channel_id=1, source_target_pairs={{1,0},{2,1},{3,2},{4,3},{5,4},{6,5},{7,6},{8,7},{9,8},{10,9},{11,1... | collective-permute-start | bytes 1572872 | tf_op jit(solution)/shard_map/ppermute | solution.py:15
  366.0 55.6 %collective-permute-start.14 = (bf16[1,128,2048]{2,1,0:T(8,128)(2,1)S(1)}, bf16[1,128,2048]{2,1,0:T(8,128)(2,1)S(1)}, u32[]{:S(2)}, u32[]{:S(2)}) collective-permute-start(bf16[1,128,2048]{2,1,0:T(8,128)(2,1)S(1)} %get-tuple-element.132), channel_id=1, source_target_pairs={{3,0},{4,1},{5,2},{6,3},{7,4},{8,5},{9,6},{10,7},{11,8},{12,9},{13... | collective-permute-start | bytes 1572872 | tf_op jit(solution)/shard_map/ppermute | solution.py:15
  373.0 49.4 %collective-permute-start.15 = (bf16[1,128,2048]{2,1,0:T(8,128)(2,1)S(1)}, bf16[1,128,2048]{2,1,0:T(8,128)(2,1)S(1)}, u32[]{:S(2)}, u32[]{:S(2)}) collective-permute-start(bf16[1,128,2048]{2,1,0:T(8,128)(2,1)S(1)} %get-tuple-element.132), channel_id=1, source_target_pairs={{4,0},{5,1},{6,2},{7,3},{8,4},{9,5},{10,6},{11,7},{12,8},{13,9},{1... | collective-permute-start | bytes 1572872 | tf_op jit(solution)/shard_map/ppermute | solution.py:15
  396.0 27.2 %collective-permute-start.16 = (bf16[1,128,2048]{2,1,0:T(8,128)(2,1)S(1)}, bf16[1,128,2048]{2,1,0:T(8,128)(2,1)S(1)}, u32[]{:S(2)}, u32[]{:S(2)}) collective-permute-start(bf16[1,128,2048]{2,1,0:T(8,128)(2,1)S(1)} %get-tuple-element.132), channel_id=1, source_target_pairs={{5,0},{6,1},{7,2},{8,3},{9,4},{10,5},{11,6},{12,7},{13,8},{14,9},{... | collective-permute-start | bytes 1572872 | tf_op jit(solution)/shard_map/ppermute | solution.py:15
  424.1 58.7 %copy-start.5 = (bf16[128,1024]{1,0:T(8,128)(2,1)S(1)}, bf16[128,1024]{1,0:T(8,128)(2,1)}, u32[]{:S(2)}) copy-start(bf16[128,1024]{1,0:T(8,128)(2,1)} %copy-done.4) | copy-start | bytes 786436
  424.1 0.7 copy-start.6
  440.8 7.3 %copy-start.7 = (bf16[128,1024]{1,0:T(8,128)(2,1)S(1)}, bf16[128,1024]{1,0:T(8,128)(2,1)}, u32[]{:S(2)}) copy-start(bf16[128,1024]{1,0:T(8,128)(2,1)} %copy-done.6) | copy-start | bytes 786436 | tf_op jit(solution)/shard_map/cond
  463.7 8.2 %copy-start.3 = (bf16[1,1024,1024]{2,1,0:T(8,128)(2,1)S(1)}, bf16[1,1024,1024]{2,1,0:T(8,128)(2,1)}, u32[]{:S(2)}) copy-start(bf16[1,1024,1024]{2,1,0:T(8,128)(2,1)} %get-tuple-element.122) | copy-start | bytes 6291460 | tf_op jit(solution)/shard_map/cond
Sparse Core Ops, SparseCore 0:
  10.1 157.5 all-gather.2
  170.5 111.0 all-gather.4
where the time goes:
time: 491 us; the launch traced here: 490 us
  waiting for transfers between devices  342 us (70%)
  starting transfers between devices  46.8 us (10%)
  local copies, waits for them, and re-layouts  45.5 us (9%)
  matrix products  26.8 us (5%)
  other arithmetic  14.5 us (3%)
  between operations  13.7 us (3%)
    ppermute x17, waiting for transfers between devices, from_behind(): return lax.ppermute(block, axis, route)  159 us
    all_gather x1, waiting for transfers between devices, local(): lax.all_gather(w_down, 'seq', axis=1, tiled=True)  114 us
    all_gather x1, waiting for transfers between devices, local(): lax.all_gather(w_up, 'seq', axis=1, tiled=True)  67.9 us
    ppermute x17, starting transfers between devices, from_behind(): return lax.ppermute(block, axis, route)  46.7 us
    unnamed x30, local copies, waits for them, and re-layouts  19.1 us
    another operation x6, local copies, waits for them, and re-layouts  12.3 us
    dot_general x1, matrix products, finish(): jnp.dot(hidden, down_weight, preferred_element_type=jnp.float32)  10 us
  transfers between devices with their start and end apart: 19, of which 11 were waited for; matrix products, arithmetic and copies ran while one was open for 4% of the time, Pallas kernels for 0%

commit v1 on v0

--- a/solution.py
+++ b/solution.py
@@ -7,6 +7,19 @@
 HEADS = 16
 BLK = 128
 ROW = 4
+
+
+def gather_around(x, axis, dim):
+    ways = lax.axis_size(axis)
+    up = [(d, (d + 1) % ways) for d in range(ways)]
+    down = [(d, (d - 1) % ways) for d in range(ways)]
+    earlier, later = ([x], [x])
+    for _ in range(ways // 2):
+        earlier.append(lax.ppermute(earlier[-1], axis, up))
+    for _ in range((ways - 1) // 2):
+        later.append(lax.ppermute(later[-1], axis, down))
+    line = jnp.concatenate([*earlier[::-1], *later[1:]], axis=dim)
+    return jnp.roll(line, (lax.axis_index(axis) - ways // 2) * x.shape[dim], axis=dim)
 
 
 def from_behind(block, axis, distance):
@@ -133,7 +146,7 @@
     device = lax.axis_index("seq")
     ticks = graphs + sections - 1
     up_whole, down_whole = (
-        lax.all_gather(w_up, "seq", axis=1, tiled=True),
+        gather_around(w_up, "seq", 1),
         lax.all_gather(w_down, "seq", axis=1, tiled=True),
     )
     results = jnp.zeros((1, graphs, tok_rows, width), jnp.bfloat16)

time: 491 us -> 564 us (1.15)
  starting transfers between devices: 46.8 us -> 120 us
  waiting for transfers between devices: 342 us -> 303 us
  local copies, waits for them, and re-layouts: 45.5 us -> 80.2 us
    ppermute x0 -> x15, waiting for transfers between devices: none -> 153 us  [the longest x8 133 us: gather_around(): earlier.append(lax.ppermute(earlier[-1], axis, up))]
    all_gather x1, waiting for transfers between devices: 114 us -> 0.01 us  [local(): lax.all_gather(w_down, 'seq', axis=1, tiled=True)]
    all_gather x1 -> x0, waiting for transfers between devices: 67.9 us -> none  [local(): lax.all_gather(w_up, 'seq', axis=1, tiled=True)]
    ppermute x17, starting transfers between devices: 46.7 us -> 89.3 us  [from_behind(): return lax.ppermute(block, axis, route)]
    ppermute x0 -> x15, starting transfers between devices: none -> 30.8 us  [the longest x7 17.7 us: gather_around(): later.append(lax.ppermute(later[-1], axis, down))]
    unnamed x30 -> x69, local copies, waits for them, and re-layouts: 19.1 us -> 45.3 us
    ppermute x17, waiting for transfers between devices: 159 us -> 149 us  [from_behind(): return lax.ppermute(block, axis, route)]
    dynamic_slice x0 -> x1, local copies, waits for them, and re-layouts: none -> 7.63 us  [gather_around(): jnp.roll(line, (lax.axis_index(axis) - ways // 2) * x.shape[dim], axis=dim)]
  transfers between devices with their start and end apart: 19 -> 33, of which waited for: 11 -> 18; matrix products, arithmetic and copies ran while one was open for 4% -> 10% of each run, Pallas kernels for 0% -> 0%
where the time goes in v1:
time: 564 us; the launch traced here: 559 us
  waiting for transfers between devices  303 us (54%)
  starting transfers between devices  120 us (21%)
  local copies, waits for them, and re-layouts  80.2 us (14%)
  matrix products  26.8 us (5%)
  other arithmetic  14.5 us (3%)
  between operations  13.8 us (2%)
    ppermute x17, waiting for transfers between devices, from_behind(): return lax.ppermute(block, axis, route)  149 us
    ppermute x8, waiting for transfers between devices, gather_around(): earlier.append(lax.ppermute(earlier[-1], axis, up))  133 us
    ppermute x17, starting transfers between devices, from_behind(): return lax.ppermute(block, axis, route)  89.3 us
    unnamed x69, local copies, waits for them, and re-layouts  45.3 us
    ppermute x7, waiting for transfers between devices, gather_around(): later.append(lax.ppermute(later[-1], axis, down))  20.5 us
    ppermute x7, starting transfers between devices, gather_around(): later.append(lax.ppermute(later[-1], axis, down))  17.7 us
    another operation x6, local copies, waits for them, and re-layouts  13.1 us
    ppermute x8, starting transfers between devices, gather_around(): earlier.append(lax.ppermute(earlier[-1], axis, up))  13.1 us
  transfers between devices with their start and end apart: 33, of which 18 were waited for; matrix products, arithmetic and copies ran while one was open for 10% of the time, Pallas kernels for 0%

profile of v1, /device:TPU:9, one launch (start us, length us, event | category | flops | bytes accessed | tf_op | source)
XLA Modules:
  0.0 559.2 jit_solution(14230796858118847641)
XLA Ops:
  8.5 13.6 %collective-permute-done.8 = bf16[1,256,1024]{2,1,0:T(8,128)(2,1)S(1)} collective-permute-done((bf16[1,256,1024]{2,1,0:T(8,128)(2,1)}, bf16[1,256,1024]{2,1,0:T(8,128)(2,1)S(1)}, u32[]{:S(2)}, u32[]{:S(2)}) %collective-permute-start.8) | collective-permute-done | bytes 524320 | tf_op jit(solution)/shard_map/ppermute | solution.py:18
  22.1 3.3 collective-permute-start.16
  25.4 21.2 %collective-permute-done.9 = bf16[1,256,1024]{2,1,0:T(8,128)(2,1)S(1)} collective-permute-done((bf16[1,256,1024]{2,1,0:T(8,128)(2,1)S(1)}, bf16[1,256,1024]{2,1,0:T(8,128)(2,1)S(1)}, u32[]{:S(2)}, u32[]{:S(2)}) %collective-permute-start.9) | collective-permute-done | bytes 524320 | tf_op jit(solution)/shard_map/ppermute | solution.py:18
  46.6 2.3 collective-permute-start.10
  50.0 32.5 %collective-permute-done.10 = bf16[1,256,1024]{2,1,0:T(8,128)(2,1)} collective-permute-done((bf16[1,256,1024]{2,1,0:T(8,128)(2,1)S(1)}, bf16[1,256,1024]{2,1,0:T(8,128)(2,1)}, u32[]{:S(2)}, u32[]{:S(2)}) %collective-permute-start.10) | collective-permute-done | bytes 524320 | tf_op jit(solution)/shard_map/ppermute | solution.py:18
  82.5 2.3 collective-permute-start.11
  86.7 3.6 collective-permute-start
  90.4 2.3 collective-permute-start.1
  92.7 4.0 collective-permute-start.2
  98.0 16.0 %collective-permute-done.11 = bf16[1,256,1024]{2,1,0:T(8,128)(2,1)} collective-permute-done((bf16[1,256,1024]{2,1,0:T(8,128)(2,1)}, bf16[1,256,1024]{2,1,0:T(8,128)(2,1)}, u32[]{:S(2)}, u32[]{:S(2)}) %collective-permute-start.11) | collective-permute-done | bytes 524320 | tf_op jit(solution)/shard_map/ppermute | solution.py:18
  114.0 2.8 collective-permute-start.12
  116.8 1.9 collective-permute-start.3
  119.8 19.1 %collective-permute-start.4 = (bf16[1,128,2048]{2,1,0:T(8,128)(2,1)}, bf16[1,128,2048]{2,1,0:T(8,128)(2,1)S(1)}, u32[]{:S(2)}, u32[]{:S(2)}) collective-permute-start(bf16[1,128,2048]{2,1,0:T(8,128)(2,1)} %get-tuple-element.130), channel_id=1, source_target_pairs={{1,0},{2,1},{3,2},{4,3},{5,4},{6,5},{7,6},{8,7},{9,8},{10,9},{11,1... | collective-permute-start | bytes 1572872 | tf_op jit(solution)/shard_map/ppermute | solution.py:28
  139.0 8.5 %collective-permute-done.2 = bf16[1,128,2048]{2,1,0:T(8,128)(2,1)S(1)} collective-permute-done((bf16[1,128,2048]{2,1,0:T(8,128)(2,1)}, bf16[1,128,2048]{2,1,0:T(8,128)(2,1)S(1)}, u32[]{:S(2)}, u32[]{:S(2)}) %collective-permute-start.2) | collective-permute-done | bytes 524320 | tf_op jit(solution)/shard_map/ppermute | solution.py:28
  147.5 1.9 collective-permute-start.5
  149.4 12.1 %collective-permute-start.19 = (bf16[1,256,1024]{2,1,0:T(8,128)(2,1)S(1)}, bf16[1,256,1024]{2,1,0:T(8,128)(2,1)S(1)}, u32[]{:S(2)}, u32[]{:S(2)}) collective-permute-start(bf16[1,256,1024]{2,1,0:T(8,128)(2,1)S(1)} %collective-permute-done.18), channel_id=1, source_target_pairs={{0,15},{1,0},{2,1},{3,2},{4,3},{5,4},{6,5},{7,6},{8,7},{9,8},{10,9... | collective-permute-start | bytes 1572872 | tf_op jit(solution)/shard_map/ppermute | solution.py:20
  161.5 19.1 %collective-permute-done.12 = bf16[1,256,1024]{2,1,0:T(8,128)(2,1)S(1)} collective-permute-done((bf16[1,256,1024]{2,1,0:T(8,128)(2,1)}, bf16[1,256,1024]{2,1,0:T(8,128)(2,1)S(1)}, u32[]{:S(2)}, u32[]{:S(2)}) %collective-permute-start.12) | collective-permute-done | bytes 524320 | tf_op jit(solution)/shard_map/ppermute | solution.py:18
  180.7 21.4 %collective-permute-done.3 = bf16[1,128,2048]{2,1,0:T(8,128)(2,1)S(1)} collective-permute-done((bf16[1,128,2048]{2,1,0:T(8,128)(2,1)}, bf16[1,128,2048]{2,1,0:T(8,128)(2,1)S(1)}, u32[]{:S(2)}, u32[]{:S(2)}) %collective-permute-start.3) | collective-permute-done | bytes 524320 | tf_op jit(solution)/shard_map/ppermute | solution.py:28
  202.1 5.9 %collective-permute-start.6 = (bf16[1,128,2048]{2,1,0:T(8,128)(2,1)}, bf16[1,128,2048]{2,1,0:T(8,128)(2,1)S(1)}, u32[]{:S(2)}, u32[]{:S(2)}) collective-permute-start(bf16[1,128,2048]{2,1,0:T(8,128)(2,1)} %get-tuple-element.130), channel_id=1, source_target_pairs={{4,0},{5,1},{6,2},{7,3},{8,4},{9,5},{10,6},{11,7},{12,8},{13,9},{1... | collective-permute-start | bytes 1572872 | tf_op jit(solution)/shard_map/ppermute | solution.py:28
  208.0 8.8 %collective-permute-done.19 = bf16[1,256,1024]{2,1,0:T(8,128)(2,1)S(1)} collective-permute-done((bf16[1,256,1024]{2,1,0:T(8,128)(2,1)S(1)}, bf16[1,256,1024]{2,1,0:T(8,128)(2,1)S(1)}, u32[]{:S(2)}, u32[]{:S(2)}) %collective-permute-start.19) | collective-permute-done | bytes 524320 | tf_op jit(solution)/shard_map/ppermute | solution.py:20
  216.8 8.7 %collective-permute-done.13 = bf16[1,256,1024]{2,1,0:T(8,128)(2,1)S(1)} collective-permute-done((bf16[1,256,1024]{2,1,0:T(8,128)(2,1)S(1)}, bf16[1,256,1024]{2,1,0:T(8,128)(2,1)S(1)}, u32[]{:S(2)}, u32[]{:S(2)}) %collective-permute-start.13) | collective-permute-done | bytes 524320 | tf_op jit(solution)/shard_map/ppermute | solution.py:18
  225.5 2.2 collective-permute-start.14
  228.8 1.4 collective-permute-start.7
  230.4 8.9 %collective-permute-done.20 = bf16[1,256,1024]{2,1,0:T(8,128)(2,1)S(1)} collective-permute-done((bf16[1,256,1024]{2,1,0:T(8,128)(2,1)S(1)}, bf16[1,256,1024]{2,1,0:T(8,128)(2,1)S(1)}, u32[]{:S(2)}, u32[]{:S(2)}) %collective-permute-start.20) | collective-permute-done | bytes 524320 | tf_op jit(solution)/shard_map/ppermute | solution.py:20
  239.3 10.0 %collective-permute-done.14 = bf16[1,256,1024]{2,1,0:T(8,128)(2,1)S(1)} collective-permute-done((bf16[1,256,1024]{2,1,0:T(8,128)(2,1)S(1)}, bf16[1,256,1024]{2,1,0:T(8,128)(2,1)S(1)}, u32[]{:S(2)}, u32[]{:S(2)}) %collective-permute-start.14) | collective-permute-done | bytes 524320 | tf_op jit(solution)/shard_map/ppermute | solution.py:18
  249.3 2.2 collective-permute-start.15
  251.6 18.5 %collective-permute-done.7 = bf16[1,128,2048]{2,1,0:T(8,128)(2,1)S(1)} collective-permute-done((bf16[1,128,2048]{2,1,0:T(8,128)(2,1)}, bf16[1,128,2048]{2,1,0:T(8,128)(2,1)S(1)}, u32[]{:S(2)}, u32[]{:S(2)}) %collective-permute-start.7) | collective-permute-done | bytes 524320 | tf_op jit(solution)/shard_map/ppermute | solution.py:28
  270.1 2.8 collective-permute-done.21
  273.0 11.4 %collective-permute-done.15 = bf16[1,256,1024]{2,1,0:T(8,128)(2,1)S(1)} collective-permute-done((bf16[1,256,1024]{2,1,0:T(8,128)(2,1)S(1)}, bf16[1,256,1024]{2,1,0:T(8,128)(2,1)S(1)}, u32[]{:S(2)}, u32[]{:S(2)}) %collective-permute-start.15) | collective-permute-done | bytes 524320 | tf_op jit(solution)/shard_map/ppermute | solution.py:18
  287.7 1.9 constant_dynamic-update-slice_fusion.36
  289.6 1.9 constant_dynamic-update-slice_fusion.35
  294.0 1.9 constant_dynamic-update-slice_fusion.31
  295.9 1.9 constant_dynamic-update-slice_fusion.30
  305.4 1.9 constant_dynamic-update-slice_fusion.20
  307.2 1.9 constant_dynamic-update-slice_fusion.19
  311.6 1.9 constant_dynamic-update-slice_fusion.15
  313.5 1.9 constant_dynamic-update-slice_fusion.14
  319.6 7.6 %constant_dynamic-slice_fusion = bf16[1,4096,1024]{2,1,0:T(8,128)(2,1)} fusion(bf16[1,8192,1024]{2,1,0:T(8,128)(2,1)} %constant_dynamic-update-slice_fusion.9, s32[]{:T(128)S(6)} %select_n.71), kind=kLoop, calls=%fused_computation.199 | loop fusion | bytes 16777220 | tf_op jit(solution)/shard_map/jit(_roll_dynamic)/dynamic_slice | solution.py:22
  327.5 1.3 collective-permute-start.23
  328.9 61.1 %collective-permute-done.23 = bf16[128,1024]{1,0:T(8,128)(2,1)S(1)} collective-permute-done((bf16[128,1024]{1,0:T(8,128)(2,1)S(1)}, bf16[128,1024]{1,0:T(8,128)(2,1)S(1)}, u32[]{:S(2)}, u32[]{:S(2)}) %collective-permute-start.23) | collective-permute-done | bytes 262176 | tf_op jit(solution)/shard_map/ppermute | solution.py:28
  391.0 5.0 conditional.6
  391.1 2.2 fusion.30
  393.4 2.1 fusion.33
  396.0 25.2 %collective-permute-start.24 = (bf16[1,128,2048]{2,1,0:T(8,128)(2,1)S(1)}, bf16[1,128,2048]{2,1,0:T(8,128)(2,1)S(1)}, u32[]{:S(2)}, u32[]{:S(2)}) collective-permute-start(bf16[1,128,2048]{2,1,0:T(8,128)(2,1)S(1)} %get-tuple-element.132), channel_id=1, source_target_pairs={{0,5},{1,6},{2,7},{3,8},{4,9},{5,10},{6,11},{7,12},{8,13},{9,14},{... | collective-permute-start | bytes 1572872 | tf_op jit(solution)/shard_map/ppermute | solution.py:28
  421.2 1.9 collective-permute-start.25
  423.2 8.5 %collective-permute-start.26 = (bf16[1,128,2048]{2,1,0:T(8,128)(2,1)S(1)}, bf16[1,128,2048]{2,1,0:T(8,128)(2,1)S(1)}, u32[]{:S(2)}, u32[]{:S(2)}) collective-permute-start(bf16[1,128,2048]{2,1,0:T(8,128)(2,1)S(1)} %get-tuple-element.132), channel_id=1, source_target_pairs={{0,3},{1,4},{2,5},{3,6},{4,7},{5,8},{6,9},{7,10},{8,11},{9,12},{10... | collective-permute-start | bytes 1572872 | tf_op jit(solution)/shard_map/ppermute | solution.py:28
  431.6 1.9 collective-permute-start.27
  433.6 5.2 collective-permute-start.28
  438.8 1.9 collective-permute-start.29
  441.5 1.9 collective-permute-start.30
  444.3 23.7 %collective-permute-done.26 = bf16[1,128,2048]{2,1,0:T(8,128)(2,1)S(1)} collective-permute-done((bf16[1,128,2048]{2,1,0:T(8,128)(2,1)S(1)}, bf16[1,128,2048]{2,1,0:T(8,128)(2,1)S(1)}, u32[]{:S(2)}, u32[]{:S(2)}) %collective-permute-start.26) | collective-permute-done | bytes 524320 | tf_op jit(solution)/shard_map/ppermute | solution.py:28
  470.9 13.3 %collective-permute-done.27 = bf16[1,128,2048]{2,1,0:T(8,128)(2,1)S(1)} collective-permute-done((bf16[1,128,2048]{2,1,0:T(8,128)(2,1)S(1)}, bf16[1,128,2048]{2,1,0:T(8,128)(2,1)S(1)}, u32[]{:S(2)}, u32[]{:S(2)}) %collective-permute-start.27) | collective-permute-done | bytes 524320 | tf_op jit(solution)/shard_map/ppermute | solution.py:28
  485.9 2.8 collective-permute-done.28
  493.0 58.6 %conditional.7 = (bf16[128,1024]{1,0:T(8,128)(2,1)S(1)}) conditional(s32[]{:T(128)} %convert_element_type.100, () %tuple.42, (bf16[128,1024]{1,0:T(8,128)(2,1)S(1)}, bf16[11,128,2048]{2,1,0:T(8,128)(2,1)}, s32[]{:T(128)}, s32[1,9]{1,0:T(1,128)S(1)}, s32[1]{0:T(128)}, /*index=5*/bf16[128,1024]{1,0:T(8,128)(2,1)S(1)}, ...), branch_computations={%region_11.13_spmd, %region_12.17_spmd} | conditional | flops 3047426304 | bytes 114586176 | solution.py:190
  493.7 5.2 fusion.164
  498.9 4.1 gather_fusion.2
  503.0 2.3 gather_fusion.3
  505.3 4.3 bitcast_select_fusion.3
  509.6 7.3 %reshape.288 = bf16[1152,16,64]{2,1,0:T(8,128)(2,1)} reshape(bf16[1,9,128,1024]{3,2,1,0:T(8,128)(2,1)} %get-tuple-element.189) | data formatting | bytes 4718592 | tf_op jit(solution)/shard_map/reshape.89
  517.1 3.2 fusion.111
  521.1 6.7 %fusion.165 = (f32[16,128]{1,0:T(8,128)S(1)}, f32[16,128,1152]{1,2,0:T(8,128)}) fusion(f32[16,1152,128]{2,1,0:T(8,128)S(1)} %fusion.111, pred[1152]{0:T(1024)(128)(4,1)S(1)} %broadcast_bitcast_fusion.1), kind=kOutput, calls=%fused_computation.203 | output fusion | flops 14156927 | bytes 18883712 | tf_op jit(solution)/shard_map/cond/branch_1_fun/sub | solution.py:55
  527.7 4.7 reshape.287
  532.5 8.2 %fusion.141 = bf16[16,64,128]{2,1,0:T(8,128)(2,1)S(1)} fusion(f32[16,128,1152]{1,2,0:T(8,128)} %get-tuple-element.191, f32[16,128]{1,0:T(8,128)S(1)} %get-tuple-element.190, bf16[1152,16,64]{2,1,0:T(8,128)(2,1)} %reshape.287), kind=kOutput, calls=%fused_computation.123 | convolution fusion | flops 306839552 | bytes 12066816 | tf_op jit(solution)/shard_map/cond/branch_1_fun/bhqk,bkhd->bqhd/dot_general | solution.py:110
  541.3 10.0 %fusion.138 = bf16[128,1024]{1,0:T(8,128)(2,1)S(1)} fusion(f32[128,1024]{1,0:T(8,128)S(1)} %get-tuple-element.193, bf16[1,4096,1024]{2,1,0:T(8,128)(2,1)} %get-tuple-element.125, bf16[1,4096,1024]{2,1,0:T(8,128)(2,1)} %get-tuple-element.124, f32[1024]{0:T(1024)S(1)} %bitcast.180, f32[128]{0:T(128)S(1)} %add_rsqrt_fusion.3), kind=kOutput, calls=%fused_computation.122 | convolution fusion | flops 2152857600 | bytes 17568256 | tf_op jit(solution)/shard_map/cond/branch_1_fun/dot_general | solution.py:124
  (117 shorter events, 45.3 us)
Async XLA Ops:
  6.5 320.7 %all-gather.2.cloned.1.call-start = ((), (), s32[]{:S(2)}) async-start(), calls=%async_computation | async-start | bytes 8912896 | tf_op jit(solution)/shard_map/all_gather | solution.py:150
  7.3 14.9 %collective-permute-start.8 = (bf16[1,256,1024]{2,1,0:T(8,128)(2,1)}, bf16[1,256,1024]{2,1,0:T(8,128)(2,1)S(1)}, u32[]{:S(2)}, u32[]{:S(2)}) collective-permute-start(bf16[1,256,1024]{2,1,0:T(8,128)(2,1)} %param.33), channel_id=1, source_target_pairs={{0,1},{1,2},{2,3},{3,4},{4,5},{5,6},{6,7},{7,8},{8,9},{9,10},{10,1... | collective-permute-start | bytes 1572872 | tf_op jit(solution)/shard_map/ppermute | solution.py:18
  22.1 24.5 %collective-permute-start.9 = (bf16[1,256,1024]{2,1,0:T(8,128)(2,1)S(1)}, bf16[1,256,1024]{2,1,0:T(8,128)(2,1)S(1)}, u32[]{:S(2)}, u32[]{:S(2)}) collective-permute-start(bf16[1,256,1024]{2,1,0:T(8,128)(2,1)S(1)} %collective-permute-done.8), channel_id=1, source_target_pairs={{0,1},{1,2},{2,3},{3,4},{4,5},{5,6},{6,7},{7,8},{8,9},{9,10},{10,1... | collective-permute-start | bytes 1572872 | tf_op jit(solution)/shard_map/ppermute | solution.py:18
  22.1 26.8 %collective-permute-start.16 = (bf16[1,256,1024]{2,1,0:T(8,128)(2,1)}, bf16[1,256,1024]{2,1,0:T(8,128)(2,1)}, u32[]{:S(2)}, u32[]{:S(2)}) collective-permute-start(bf16[1,256,1024]{2,1,0:T(8,128)(2,1)} %param.33), channel_id=1, source_target_pairs={{0,15},{1,0},{2,1},{3,2},{4,3},{5,4},{6,5},{7,6},{8,7},{9,8},{10,9... | collective-permute-start | bytes 1572872 | tf_op jit(solution)/shard_map/ppermute | solution.py:20
  46.6 39.2 %copy-start.6 = (bf16[1,256,1024]{2,1,0:T(8,128)(2,1)}, bf16[1,256,1024]{2,1,0:T(8,128)(2,1)S(1)}, u32[]{:S(2)}) copy-start(bf16[1,256,1024]{2,1,0:T(8,128)(2,1)S(1)} %collective-permute-done.9) | copy-start | bytes 1572868
  46.6 35.9 %collective-permute-start.10 = (bf16[1,256,1024]{2,1,0:T(8,128)(2,1)S(1)}, bf16[1,256,1024]{2,1,0:T(8,128)(2,1)}, u32[]{:S(2)}, u32[]{:S(2)}) collective-permute-start(bf16[1,256,1024]{2,1,0:T(8,128)(2,1)S(1)} %collective-permute-done.9), channel_id=1, source_target_pairs={{0,1},{1,2},{2,3},{3,4},{4,5},{5,6},{6,7},{7,8},{8,9},{9,10},{10,1... | collective-permute-start | bytes 1572872 | tf_op jit(solution)/shard_map/ppermute | solution.py:18
  48.9 47.8 %collective-permute-start.17 = (bf16[1,256,1024]{2,1,0:T(8,128)(2,1)}, bf16[1,256,1024]{2,1,0:T(8,128)(2,1)}, u32[]{:S(2)}, u32[]{:S(2)}) collective-permute-start(bf16[1,256,1024]{2,1,0:T(8,128)(2,1)} %collective-permute-done.16), channel_id=1, source_target_pairs={{0,15},{1,0},{2,1},{3,2},{4,3},{5,4},{6,5},{7,6},{8,7},{9,8},{10,9... | collective-permute-start | bytes 1572872 | tf_op jit(solution)/shard_map/ppermute | solution.py:20
  82.5 31.5 %collective-permute-start.11 = (bf16[1,256,1024]{2,1,0:T(8,128)(2,1)}, bf16[1,256,1024]{2,1,0:T(8,128)(2,1)}, u32[]{:S(2)}, u32[]{:S(2)}) collective-permute-start(bf16[1,256,1024]{2,1,0:T(8,128)(2,1)} %collective-permute-done.10), channel_id=1, source_target_pairs={{0,1},{1,2},{2,3},{3,4},{4,5},{5,6},{6,7},{7,8},{8,9},{9,10},{10,1... | collective-permute-start | bytes 1572872 | tf_op jit(solution)/shard_map/ppermute | solution.py:18
  86.7 30.1 %collective-permute-start = (bf16[1,128,2048]{2,1,0:T(8,128)(2,1)}, bf16[1,128,2048]{2,1,0:T(8,128)(2,1)}, u32[]{:S(2)}, u32[]{:S(2)}) collective-permute-start(bf16[1,128,2048]{2,1,0:T(8,128)(2,1)} %get-tuple-element.130), channel_id=1, source_target_pairs={{0,5},{1,6},{2,7},{3,8},{4,9},{5,10},{6,11},{7,12},{8,13},{9,14},{... | collective-permute-start | bytes 1572872 | tf_op jit(solution)/shard_map/ppermute | solution.py:28
  90.4 29.4 %collective-permute-start.1 = (bf16[1,128,2048]{2,1,0:T(8,128)(2,1)}, bf16[1,128,2048]{2,1,0:T(8,128)(2,1)S(1)}, u32[]{:S(2)}, u32[]{:S(2)}) collective-permute-start(bf16[1,128,2048]{2,1,0:T(8,128)(2,1)} %get-tuple-element.130), channel_id=1, source_target_pairs={{0,4},{1,5},{2,6},{3,7},{4,8},{5,9},{6,10},{7,11},{8,12},{9,13},{1... | collective-permute-start | bytes 1572872 | tf_op jit(solution)/shard_map/ppermute | solution.py:28
  92.7 54.8 %collective-permute-start.2 = (bf16[1,128,2048]{2,1,0:T(8,128)(2,1)}, bf16[1,128,2048]{2,1,0:T(8,128)(2,1)S(1)}, u32[]{:S(2)}, u32[]{:S(2)}) collective-permute-start(bf16[1,128,2048]{2,1,0:T(8,128)(2,1)} %get-tuple-element.130), channel_id=1, source_target_pairs={{0,3},{1,4},{2,5},{3,6},{4,7},{5,8},{6,9},{7,10},{8,11},{9,12},{10... | collective-permute-start | bytes 1572872 | tf_op jit(solution)/shard_map/ppermute | solution.py:28
  96.7 52.7 %collective-permute-start.18 = (bf16[1,256,1024]{2,1,0:T(8,128)(2,1)}, bf16[1,256,1024]{2,1,0:T(8,128)(2,1)S(1)}, u32[]{:S(2)}, u32[]{:S(2)}) collective-permute-start(bf16[1,256,1024]{2,1,0:T(8,128)(2,1)} %collective-permute-done.17), channel_id=1, source_target_pairs={{0,15},{1,0},{2,1},{3,2},{4,3},{5,4},{6,5},{7,6},{8,7},{9,8},{10,9... | collective-permute-start | bytes 1572872 | tf_op jit(solution)/shard_map/ppermute | solution.py:20
  114.0 66.6 %collective-permute-start.12 = (bf16[1,256,1024]{2,1,0:T(8,128)(2,1)}, bf16[1,256,1024]{2,1,0:T(8,128)(2,1)S(1)}, u32[]{:S(2)}, u32[]{:S(2)}) collective-permute-start(bf16[1,256,1024]{2,1,0:T(8,128)(2,1)} %collective-permute-done.11), channel_id=1, source_target_pairs={{0,1},{1,2},{2,3},{3,4},{4,5},{5,6},{6,7},{7,8},{8,9},{9,10},{10,1... | collective-permute-start | bytes 1572872 | tf_op jit(solution)/shard_map/ppermute | solution.py:18
  116.8 85.3 %collective-permute-start.3 = (bf16[1,128,2048]{2,1,0:T(8,128)(2,1)}, bf16[1,128,2048]{2,1,0:T(8,128)(2,1)S(1)}, u32[]{:S(2)}, u32[]{:S(2)}) collective-permute-start(bf16[1,128,2048]{2,1,0:T(8,128)(2,1)} %get-tuple-element.130), channel_id=1, source_target_pairs={{0,1},{1,2},{2,3},{3,4},{4,5},{5,6},{6,7},{7,8},{8,9},{9,10},{10,1... | collective-permute-start | bytes 1572872 | tf_op jit(solution)/shard_map/ppermute | solution.py:28
  119.8 109.0 %collective-permute-start.4 = (bf16[1,128,2048]{2,1,0:T(8,128)(2,1)}, bf16[1,128,2048]{2,1,0:T(8,128)(2,1)S(1)}, u32[]{:S(2)}, u32[]{:S(2)}) collective-permute-start(bf16[1,128,2048]{2,1,0:T(8,128)(2,1)} %get-tuple-element.130), channel_id=1, source_target_pairs={{1,0},{2,1},{3,2},{4,3},{5,4},{6,5},{7,6},{8,7},{9,8},{10,9},{11,1... | collective-permute-start | bytes 1572872 | tf_op jit(solution)/shard_map/ppermute | solution.py:28
  147.5 103.9 %collective-permute-start.5 = (bf16[1,128,2048]{2,1,0:T(8,128)(2,1)}, bf16[1,128,2048]{2,1,0:T(8,128)(2,1)S(1)}, u32[]{:S(2)}, u32[]{:S(2)}) collective-permute-start(bf16[1,128,2048]{2,1,0:T(8,128)(2,1)} %get-tuple-element.130), channel_id=1, source_target_pairs={{3,0},{4,1},{5,2},{6,3},{7,4},{8,5},{9,6},{10,7},{11,8},{12,9},{13... | collective-permute-start | bytes 1572872 | tf_op jit(solution)/shard_map/ppermute | solution.py:28
  149.4 67.3 %collective-permute-start.19 = (bf16[1,256,1024]{2,1,0:T(8,128)(2,1)S(1)}, bf16[1,256,1024]{2,1,0:T(8,128)(2,1)S(1)}, u32[]{:S(2)}, u32[]{:S(2)}) collective-permute-start(bf16[1,256,1024]{2,1,0:T(8,128)(2,1)S(1)} %collective-permute-done.18), channel_id=1, source_target_pairs={{0,15},{1,0},{2,1},{3,2},{4,3},{5,4},{6,5},{7,6},{8,7},{9,8},{10,9... | collective-permute-start | bytes 1572872 | tf_op jit(solution)/shard_map/ppermute | solution.py:20
  180.6 44.9 %collective-permute-start.13 = (bf16[1,256,1024]{2,1,0:T(8,128)(2,1)S(1)}, bf16[1,256,1024]{2,1,0:T(8,128)(2,1)S(1)}, u32[]{:S(2)}, u32[]{:S(2)}) collective-permute-start(bf16[1,256,1024]{2,1,0:T(8,128)(2,1)S(1)} %collective-permute-done.12), channel_id=1, source_target_pairs={{0,1},{1,2},{2,3},{3,4},{4,5},{5,6},{6,7},{7,8},{8,9},{9,10},{10,1... | collective-permute-start | bytes 1572872 | tf_op jit(solution)/shard_map/ppermute | solution.py:18
  202.1 49.4 %collective-permute-start.6 = (bf16[1,128,2048]{2,1,0:T(8,128)(2,1)}, bf16[1,128,2048]{2,1,0:T(8,128)(2,1)S(1)}, u32[]{:S(2)}, u32[]{:S(2)}) collective-permute-start(bf16[1,128,2048]{2,1,0:T(8,128)(2,1)} %get-tuple-element.130), channel_id=1, source_target_pairs={{4,0},{5,1},{6,2},{7,3},{8,4},{9,5},{10,6},{11,7},{12,8},{13,9},{1... | collective-permute-start | bytes 1572872 | tf_op jit(solution)/shard_map/ppermute | solution.py:28
  216.8 22.5 %collective-permute-start.20 = (bf16[1,256,1024]{2,1,0:T(8,128)(2,1)S(1)}, bf16[1,256,1024]{2,1,0:T(8,128)(2,1)S(1)}, u32[]{:S(2)}, u32[]{:S(2)}) collective-permute-start(bf16[1,256,1024]{2,1,0:T(8,128)(2,1)S(1)} %collective-permute-done.19), channel_id=1, source_target_pairs={{0,15},{1,0},{2,1},{3,2},{4,3},{5,4},{6,5},{7,6},{8,7},{9,8},{10,9... | collective-permute-start | bytes 1572872 | tf_op jit(solution)/shard_map/ppermute | solution.py:20
  225.5 23.7 %collective-permute-start.14 = (bf16[1,256,1024]{2,1,0:T(8,128)(2,1)S(1)}, bf16[1,256,1024]{2,1,0:T(8,128)(2,1)S(1)}, u32[]{:S(2)}, u32[]{:S(2)}) collective-permute-start(bf16[1,256,1024]{2,1,0:T(8,128)(2,1)S(1)} %collective-permute-done.13), channel_id=1, source_target_pairs={{0,1},{1,2},{2,3},{3,4},{4,5},{5,6},{6,7},{7,8},{8,9},{9,10},{10,1... | collective-permute-start | bytes 1572872 | tf_op jit(solution)/shard_map/ppermute | solution.py:18
  228.8 62.7 %copy-start.7 = (bf16[1,256,1024]{2,1,0:T(8,128)(2,1)S(1)}, bf16[1,256,1024]{2,1,0:T(8,128)(2,1)}, u32[]{:S(2)}) copy-start(bf16[1,256,1024]{2,1,0:T(8,128)(2,1)} %copy-done.6) | copy-start | bytes 1572868
  228.8 41.2 %collective-permute-start.7 = (bf16[1,128,2048]{2,1,0:T(8,128)(2,1)}, bf16[1,128,2048]{2,1,0:T(8,128)(2,1)S(1)}, u32[]{:S(2)}, u32[]{:S(2)}) collective-permute-start(bf16[1,128,2048]{2,1,0:T(8,128)(2,1)} %get-tuple-element.130), channel_id=1, source_target_pairs={{5,0},{6,1},{7,2},{8,3},{9,4},{10,5},{11,6},{12,7},{13,8},{14,9},{... | collective-permute-start | bytes 1572872 | tf_op jit(solution)/shard_map/ppermute | solution.py:28
  230.4 62.8 %copy-start.5 = (bf16[1,256,1024]{2,1,0:T(8,128)(2,1)S(1)}, bf16[1,256,1024]{2,1,0:T(8,128)(2,1)}, u32[]{:S(2)}) copy-start(bf16[1,256,1024]{2,1,0:T(8,128)(2,1)} %param.33) | copy-start | bytes 1572868
  239.3 33.7 %collective-permute-start.21 = (bf16[1,256,1024]{2,1,0:T(8,128)(2,1)S(1)}, bf16[1,256,1024]{2,1,0:T(8,128)(2,1)S(1)}, u32[]{:S(2)}, u32[]{:S(2)}) collective-permute-start(bf16[1,256,1024]{2,1,0:T(8,128)(2,1)S(1)} %collective-permute-done.20), channel_id=1, source_target_pairs={{0,15},{1,0},{2,1},{3,2},{4,3},{5,4},{6,5},{7,6},{8,7},{9,8},{10,9... | collective-permute-start | bytes 1572872 | tf_op jit(solution)/shard_map/ppermute | solution.py:20
  249.3 35.1 %collective-permute-start.15 = (bf16[1,256,1024]{2,1,0:T(8,128)(2,1)S(1)}, bf16[1,256,1024]{2,1,0:T(8,128)(2,1)S(1)}, u32[]{:S(2)}, u32[]{:S(2)}) collective-permute-start(bf16[1,256,1024]{2,1,0:T(8,128)(2,1)S(1)} %collective-permute-done.14), channel_id=1, source_target_pairs={{0,1},{1,2},{2,3},{3,4},{4,5},{5,6},{6,7},{7,8},{8,9},{9,10},{10,1... | collective-permute-start | bytes 1572872 | tf_op jit(solution)/shard_map/ppermute | solution.py:18
  270.1 27.6 %copy-start.4 = (bf16[11,128,2048]{2,1,0:T(8,128)(2,1)}, bf16[11,128,2048]{2,1,0:T(8,128)(2,1)S(1)}, u32[]{:S(2)}) copy-start(bf16[11,128,2048]{2,1,0:T(8,128)(2,1)S(1)} %constant_dynamic-update-slice_fusion) | copy-start | bytes 17301508
  273.0 28.1 %collective-permute-start.22 = (bf16[1,256,1024]{2,1,0:T(8,128)(2,1)S(1)}, bf16[1,256,1024]{2,1,0:T(8,128)(2,1)S(1)}, u32[]{:S(2)}, u32[]{:S(2)}) collective-permute-start(bf16[1,256,1024]{2,1,0:T(8,128)(2,1)S(1)} %collective-permute-done.21), channel_id=1, source_target_pairs={{0,15},{1,0},{2,1},{3,2},{4,3},{5,4},{6,5},{7,6},{8,7},{9,8},{10,9... | collective-permute-start | bytes 1572872 | tf_op jit(solution)/shard_map/ppermute | solution.py:20
  319.6 7.6 %copy-start.14 = (s32[1,9]{1,0:T(1,128)S(1)}, s32[1,9]{1,0:T(1,128)}, u32[]{:S(2)}) copy-start(s32[1,9]{1,0:T(1,128)} %param.26) | copy-start | bytes 112
  319.6 7.6 %copy-start.15 = (f32[1,1024]{1,0:T(1,128)S(1)}, f32[1,1024]{1,0:T(1,128)}, u32[]{:S(2)}) copy-start(f32[1,1024]{1,0:T(1,128)} %param.35) | copy-start | bytes 12292
  327.3 63.7 %copy-start.12 = (f32[1,1024]{1,0:T(1,128)S(1)}, f32[1,1024]{1,0:T(1,128)}, u32[]{:S(2)}) copy-start(f32[1,1024]{1,0:T(1,128)} %param.32) | copy-start | bytes 12292
  327.5 63.4 %copy-start.8 = (bf16[128,1024]{1,0:T(8,128)(2,1)}, bf16[128,1024]{1,0:T(8,128)(2,1)S(1)}, u32[]{:S(2)}) copy-start(bf16[128,1024]{1,0:T(8,128)(2,1)S(1)} %get-tuple-element.202) | copy-start | bytes 786436
  327.5 62.4 %collective-permute-start.23 = (bf16[128,1024]{1,0:T(8,128)(2,1)S(1)}, bf16[128,1024]{1,0:T(8,128)(2,1)S(1)}, u32[]{:S(2)}, u32[]{:S(2)}) collective-permute-start(bf16[128,1024]{1,0:T(8,128)(2,1)S(1)} %get-tuple-element.202), channel_id=1, source_target_pairs={{0,16},{1,17},{2,18},{3,19},{4,20},{5,21},{6,22},{7,23},{8,24},{9,... | collective-permute-start | bytes 786440 | tf_op jit(solution)/shard_map/ppermute | solution.py:28
  391.0 4.5 copy-start.1
  396.0 42.7 %collective-permute-start.24 = (bf16[1,128,2048]{2,1,0:T(8,128)(2,1)S(1)}, bf16[1,128,2048]{2,1,0:T(8,128)(2,1)S(1)}, u32[]{:S(2)}, u32[]{:S(2)}) collective-permute-start(bf16[1,128,2048]{2,1,0:T(8,128)(2,1)S(1)} %get-tuple-element.132), channel_id=1, source_target_pairs={{0,5},{1,6},{2,7},{3,8},{4,9},{5,10},{6,11},{7,12},{8,13},{9,14},{... | collective-permute-start | bytes 1572872 | tf_op jit(solution)/shard_map/ppermute | solution.py:28
  421.2 20.3 %collective-permute-start.25 = (bf16[1,128,2048]{2,1,0:T(8,128)(2,1)S(1)}, bf16[1,128,2048]{2,1,0:T(8,128)(2,1)S(1)}, u32[]{:S(2)}, u32[]{:S(2)}) collective-permute-start(bf16[1,128,2048]{2,1,0:T(8,128)(2,1)S(1)} %get-tuple-element.132), channel_id=1, source_target_pairs={{0,4},{1,5},{2,6},{3,7},{4,8},{5,9},{6,10},{7,11},{8,12},{9,13},{1... | collective-permute-start | bytes 1572872 | tf_op jit(solution)/shard_map/ppermute | solution.py:28
  423.2 44.8 %collective-permute-start.26 = (bf16[1,128,2048]{2,1,0:T(8,128)(2,1)S(1)}, bf16[1,128,2048]{2,1,0:T(8,128)(2,1)S(1)}, u32[]{:S(2)}, u32[]{:S(2)}) collective-permute-start(bf16[1,128,2048]{2,1,0:T(8,128)(2,1)S(1)} %get-tuple-element.132), channel_id=1, source_target_pairs={{0,3},{1,4},{2,5},{3,6},{4,7},{5,8},{6,9},{7,10},{8,11},{9,12},{10... | collective-permute-start | bytes 1572872 | tf_op jit(solution)/shard_map/ppermute | solution.py:28
  431.6 52.6 %collective-permute-start.27 = (bf16[1,128,2048]{2,1,0:T(8,128)(2,1)S(1)}, bf16[1,128,2048]{2,1,0:T(8,128)(2,1)S(1)}, u32[]{:S(2)}, u32[]{:S(2)}) collective-permute-start(bf16[1,128,2048]{2,1,0:T(8,128)(2,1)S(1)} %get-tuple-element.132), channel_id=1, source_target_pairs={{0,1},{1,2},{2,3},{3,4},{4,5},{5,6},{6,7},{7,8},{8,9},{9,10},{10,1... | collective-permute-start | bytes 1572872 | tf_op jit(solution)/shard_map/ppermute | solution.py:28
  433.6 55.2 %collective-permute-start.28 = (bf16[1,128,2048]{2,1,0:T(8,128)(2,1)S(1)}, bf16[1,128,2048]{2,1,0:T(8,128)(2,1)S(1)}, u32[]{:S(2)}, u32[]{:S(2)}) collective-permute-start(bf16[1,128,2048]{2,1,0:T(8,128)(2,1)S(1)} %get-tuple-element.132), channel_id=1, source_target_pairs={{1,0},{2,1},{3,2},{4,3},{5,4},{6,5},{7,6},{8,7},{9,8},{10,9},{11,1... | collective-permute-start | bytes 1572872 | tf_op jit(solution)/shard_map/ppermute | solution.py:28
  438.8 51.7 %collective-permute-start.29 = (bf16[1,128,2048]{2,1,0:T(8,128)(2,1)S(1)}, bf16[1,128,2048]{2,1,0:T(8,128)(2,1)S(1)}, u32[]{:S(2)}, u32[]{:S(2)}) collective-permute-start(bf16[1,128,2048]{2,1,0:T(8,128)(2,1)S(1)} %get-tuple-element.132), channel_id=1, source_target_pairs={{3,0},{4,1},{5,2},{6,3},{7,4},{8,5},{9,6},{10,7},{11,8},{12,9},{13... | collective-permute-start | bytes 1572872 | tf_op jit(solution)/shard_map/ppermute | solution.py:28
  441.5 49.8 %collective-permute-start.30 = (bf16[1,128,2048]{2,1,0:T(8,128)(2,1)S(1)}, bf16[1,128,2048]{2,1,0:T(8,128)(2,1)S(1)}, u32[]{:S(2)}, u32[]{:S(2)}) collective-permute-start(bf16[1,128,2048]{2,1,0:T(8,128)(2,1)S(1)} %get-tuple-element.132), channel_id=1, source_target_pairs={{4,0},{5,1},{6,2},{7,3},{8,4},{9,5},{10,6},{11,7},{12,8},{13,9},{1... | collective-permute-start | bytes 1572872 | tf_op jit(solution)/shard_map/ppermute | solution.py:28
  468.0 24.1 %collective-permute-start.31 = (bf16[1,128,2048]{2,1,0:T(8,128)(2,1)S(1)}, bf16[1,128,2048]{2,1,0:T(8,128)(2,1)S(1)}, u32[]{:S(2)}, u32[]{:S(2)}) collective-permute-start(bf16[1,128,2048]{2,1,0:T(8,128)(2,1)S(1)} %get-tuple-element.132), channel_id=1, source_target_pairs={{5,0},{6,1},{7,2},{8,3},{9,4},{10,5},{11,6},{12,7},{13,8},{14,9},{... | collective-permute-start | bytes 1572872 | tf_op jit(solution)/shard_map/ppermute | solution.py:28
  493.0 58.7 %copy-start.9 = (bf16[128,1024]{1,0:T(8,128)(2,1)S(1)}, bf16[128,1024]{1,0:T(8,128)(2,1)}, u32[]{:S(2)}) copy-start(bf16[128,1024]{1,0:T(8,128)(2,1)} %copy-done.8) | copy-start | bytes 786436
  493.0 0.7 copy-start.10
  509.6 7.3 %copy-start.11 = (bf16[128,1024]{1,0:T(8,128)(2,1)S(1)}, bf16[128,1024]{1,0:T(8,128)(2,1)}, u32[]{:S(2)}) copy-start(bf16[128,1024]{1,0:T(8,128)(2,1)} %copy-done.10) | copy-start | bytes 786436 | tf_op jit(solution)/shard_map/cond
  532.5 8.2 %copy-start.3 = (bf16[1,1024,1024]{2,1,0:T(8,128)(2,1)S(1)}, bf16[1,1024,1024]{2,1,0:T(8,128)(2,1)}, u32[]{:S(2)}) copy-start(bf16[1,1024,1024]{2,1,0:T(8,128)(2,1)} %get-tuple-element.122) | copy-start | bytes 6291460 | tf_op jit(solution)/shard_map/cond
Sparse Core Ops, SparseCore 0:
  10.1 200.1 all-gather.1
